TPU v7x, 32 devices: a whole 2x2x4 slice. The times are simulated.
32 devices in a mesh: comp: 2 (over core), gx: 4 (over y, x), gy: 4 (over z).
Axes of the slice: x: 2, y: 2, z: 4, core: 2. Of those that a mesh axis runs over, the one named last changes fastest.
Arguments:
- state: float32 [2, 8, 96, 3072], P('comp', None, 'gx', 'gy'), may hold values from -6 to 6
- response: float32 [2, 8, 3072], P('comp'), may hold values from -0.95 to 0
- diffusion: float32 [2, 96, 3072], P('comp', 'gx', 'gy'), may hold values from 0.02 to 0.24
- land_mask: int32 [96, 3072], P('gx', 'gy'), may hold values 0 or 1
- couple_src: int32 [2, 4, 4, 16, 128], P('comp', 'gx', 'gy'), may hold values from 0 to 18431
- couple_dst: int32 [2, 4, 4, 16, 128], P('comp', 'gx', 'gy'), may hold values from 0 to 18431
- couple_weight: float32 [2, 4, 4, 16, 128], P('comp', 'gx', 'gy'), may hold values from 0.1 to 1
- couple_count: int32 [2, 4, 4, 16], P('comp', 'gx', 'gy'), may hold values from 0 to 128, as said below
Outputs:
- final_state: float32 [2, 8, 96, 3072], P('comp', None, 'gx', 'gy')
Inputs may be any that keep to these rules, and one draw needn't show every extreme that they name: `couple_count`: at most 128 live slots per ordered device pair; every sending device has one pair with exactly 128.
All inputs are finite; a program needn't handle non-finite values. No bound on the sum of `land_mask` on one device may be relied on, other than what follows from the above.
Results may differ from a plain program's by a relative error of at most 0.0095.
Values may be sent and summed in bfloat16 or wider, within the bound.
A program may use at most 128 MiB of HBM per device.

v0:
```python
import math
import jax
import jax.numpy as jnp
from jax import lax
from jax.sharding import PartitionSpec as P

FC = 4


def extended(block, sides, width):
    for axis, dim in sides:
        count = lax.axis_size(axis)
        forward = [(i, i + 1) for i in range(count - 1)]
        backward = [(target, source) for source, target in forward]
        low = lax.ppermute(
            lax.slice_in_dim(block, block.shape[dim] - width, None, axis=dim), axis, forward
        )
        high = lax.ppermute(lax.slice_in_dim(block, 0, width, axis=dim), axis, backward)
        block = jnp.concatenate([low, block, high], axis=dim)
    return block


def partner(value, axis, stride):
    mask = 2**stride
    pairs = [(source, source ^ mask) for source in range(lax.axis_size(axis))]
    return lax.ppermute(value, axis, pairs)


def make_table(cols):
    split = 64 if cols % 64 == 0 else 1
    wave_idx = jnp.arange(cols // 2, dtype=jnp.int32)[None, :]
    scale = 2.0 * math.pi / cols

    def trig(rows_idx):
        angle = (rows_idx * wave_idx % cols).astype(jnp.float32) * scale
        return (jnp.cos(angle), jnp.sin(angle))

    cos_hi, sin_hi = trig(jnp.arange(cols // split, dtype=jnp.int32)[:, None] * split)
    cos_lo, sin_lo = trig(jnp.arange(split, dtype=jnp.int32)[:, None])
    cos_hi, sin_hi = (cos_hi[:, None], sin_hi[:, None])
    cos_lo, sin_lo = (cos_lo[None], sin_lo[None])
    cos_all = cos_hi * cos_lo - sin_hi * sin_lo
    sin_all = sin_hi * cos_lo + cos_hi * sin_lo
    table = jnp.concatenate([cos_all, sin_all], axis=2).astype(jnp.bfloat16)
    return table.reshape(cols, cols)


def back_transform(filtered, table_part):
    return lax.dot_general(
        filtered, table_part, (((1,), (1,)), ((), ())), preferred_element_type=jnp.float32
    )


def circle_increment(circles, resp_part, table, scale):
    count, rows_part, cols_all = circles.shape
    spec = jnp.dot(circles.reshape(-1, cols_all), table, preferred_element_type=jnp.float32)
    spec = spec.reshape(count, rows_part, cols_all)
    filtered = (spec * resp_part[:, None, :]).astype(jnp.bfloat16)
    incr = (back_transform(filtered.reshape(-1, cols_all), table) * scale).astype(jnp.bfloat16)
    return incr.reshape(count, rows_part, cols_all)


def diffuse(fields, rate):
    padded = extended(fields.astype(jnp.bfloat16), (("gx", 1),), 1).astype(fields.dtype)
    return fields + rate[None] * (padded[:, 2:] + padded[:, :-2] - 2.0 * fields)


def local(
    state, response, diffusion, land_mask, couple_src, couple_dst, couple_weight, couple_count
):
    levels, rows_dev, cols_dev = (state.shape[1], state.shape[2], state.shape[3])
    groups_x = lax.axis_size("gx")
    groups_y = lax.axis_size("gy")
    peers = groups_x * groups_y
    slots = couple_src.shape[4]
    cells = rows_dev * cols_dev
    cols_all = cols_dev * groups_y
    per_level = levels // groups_y
    section = lax.axis_index("comp")
    keep = jnp.where(section == 1, land_mask.astype(jnp.float32), jnp.float32(1.0))
    table = make_table(cols_all)
    scale = 2.0 / cols_all
    src_idx = couple_src.reshape(peers, slots)
    dst_idx = couple_dst.reshape(peers, slots)
    live = jnp.arange(slots, dtype=jnp.int32)[None, :] < couple_count.reshape(peers, 1)
    weights = jnp.where(live, couple_weight.reshape(peers, slots), jnp.float32(0.0))
    first_level = lax.axis_index("gy") * per_level
    resp_mine = lax.dynamic_slice_in_dim(response[0], first_level, per_level, 0)
    rate = diffusion[0]
    fields = state[0]
    surface = fields[:FC].reshape(FC, cells)
    outgoing = jnp.transpose(surface[:, src_idx] * weights[None], (1, 0, 2))
    crossed = partner(outgoing, "comp", 0)
    arrived = lax.all_to_all(crossed, ("gx", "gy"), split_axis=0, concat_axis=0, tiled=True)
    incoming = jnp.transpose(arrived, (1, 0, 2))
    surface = surface.at[:, dst_idx].add(incoming)
    surf = surface.reshape(FC, rows_dev, cols_dev)
    fields = jnp.concatenate([surf, fields[FC:]], axis=0)
    grid_bf = fields.astype(jnp.bfloat16)
    circles = lax.all_to_all(grid_bf, "gy", split_axis=0, concat_axis=2, tiled=True)
    incr = circle_increment(circles, resp_mine, table, scale)
    incr = lax.all_to_all(incr, "gy", split_axis=2, concat_axis=0, tiled=True)
    fields = fields + incr.astype(jnp.float32)
    fields = diffuse(fields, rate) * keep[None]
    return fields[None]


def solution(mesh):
    return jax.shard_map(
        local,
        mesh=mesh,
        in_specs=(
            P("comp", None, "gx", "gy"),
            P("comp", None, None),
            P("comp", "gx", "gy"),
            P("gx", "gy"),
            P("comp", "gx", "gy", None, None),
            P("comp", "gx", "gy", None, None),
            P("comp", "gx", "gy", None, None),
            P("comp", "gx", "gy", None),
        ),
        out_specs=P("comp", None, "gx", "gy"),
        check_vma=False,
    )
```

profile of v0, /device:TPU:4, one launch (start us, length us, event | category | flops | bytes accessed | tf_op | source)
XLA Modules:
  0.0 130.0 jit_solution(9404093053873846128)
XLA Ops:
  0.0 0.0 copy-start
  0.0 0.0 copy-start.5
  0.0 0.0 copy-start.4
  0.0 1.1 fusion.37
  1.2 0.0 copy-start.1
  1.2 5.7 %copy.20 = f32[1,4,24,768]{1,3,2,0:T(8,128)} copy(f32[1,4,24,768]{3,2,1,0:T(8,128)S(1)} %get-tuple-element.7) | data formatting | bytes 589824 | tf_op jit(solution)/shard_map/slice | solution.py:91
  6.9 0.0 copy-done.2
  6.9 9.1 %gather_fusion = f32[2048,4]{1,0:T(8,128)S(1)} fusion(f32[4,18432]{0,1:T(8,128)} %bitcast.57, s32[2048]{0:T(1024)S(1)} %fusion.34), kind=kCustom, calls=%fused_computation | custom fusion | bytes 73728 | tf_op jit(solution)/shard_map/gather | solution.py:92
  16.0 0.3 copy.21
  16.3 0.0 copy-done.3
  16.3 0.0 copy-done.5
  16.4 0.1 bitcast_select_fusion
  16.4 0.1 collective-permute-start
  16.5 1.3 fusion.29
  17.8 1.6 %fusion.21 = (f32[64,1536]{1,0:T(8,128)S(1)}, f32[64,1536]{1,0:T(8,128)S(1)}) fusion(), kind=kLoop, calls=%fused_computation.30 | loop fusion | flops 884736 | bytes 786432 | tf_op jit(solution)/shard_map/sin | solution.py:36
  19.4 0.0 collective-permute-done
  19.4 0.6 copy.22
  20.0 7.3 %all-to-all-start = ((f32[16,4,128]{2,1,0:T(4,128)}), f32[16,4,128]{2,1,0:T(4,128)S(1)}, u32[]{:S(2)}, u32[]{:S(2)}) async-start(f32[16,4,128]{2,1,0:T(4,128)} %copy.22), calls=%async_computation | async-start | bytes 65536 | tf_op jit(solution)/shard_map/all_to_all | solution.py:94
  27.3 0.0 copy-done.4
  27.3 6.1 %all-to-all-done = f32[16,4,128]{2,1,0:T(4,128)S(1)} async-done(((f32[16,4,128]{2,1,0:T(4,128)}), f32[16,4,128]{2,1,0:T(4,128)S(1)}, u32[]{:S(2)}, u32[]{:S(2)}) %all-to-all-start) | async-done | bytes 32800 | tf_op jit(solution)/shard_map/all_to_all | solution.py:94
  33.4 0.4 copy.23
  33.7 17.6 %scatter_fusion = f32[4,18432]{0,1:T(8,128)} fusion(f32[4,18432]{0,1:T(8,128)} %bitcast.58, s32[2048]{0:T(1024)S(1)} %fusion.32, f32[2048,4]{1,0:T(8,128)S(1)} %copy.23), kind=kCustom, calls=%fused_computation.1 | custom fusion | flops 8192 | bytes 106496 | tf_op jit(solution)/shard_map/scatter-add | solution.py:96
  51.4 6.4 %copy.24 = f32[4,24,768]{2,1,0:T(8,128)S(1)} copy(f32[4,24,768]{0,2,1:T(8,128)} %bitcast.59) | data formatting | bytes 589824 | tf_op jit(solution)/shard_map/reshape | solution.py:97
  57.8 0.0 copy-done.1
  57.8 0.7 fusion.16
  58.5 3.6 %all-to-all-start.1 = ((bf16[8,24,768]{2,1,0:T(8,128)(2,1)}), bf16[8,24,768]{2,1,0:T(8,128)(2,1)S(1)}, u32[]{:S(2)}, u32[]{:S(2)}) async-start(bf16[8,24,768]{2,1,0:T(8,128)(2,1)} %fusion.16), calls=%async_computation.1 | async-start | bytes 589824 | tf_op jit(solution)/shard_map/all_to_all | solution.py:100
  62.2 9.6 %subtract_convert_fusion = (bf16[48,64,1536]{2,1,0:T(8,128)(2,1)}, bf16[48,64,1536]{2,1,0:T(8,128)(2,1)}) fusion(f32[64,1536]{1,0:T(8,128)S(1)} %get-tuple-element.13, f32[48,1536]{1,0:T(8,128)S(1)} %get-tuple-element.12, f32[64,1536]{1,0:T(8,128)S(1)} %get-tuple-element.14, f32[48,1536]{1,0:T(8,128)S(1)} %get-tuple-element.11), kind=kLoop, calls=%fused_computation.6 | loop fusion | flops 37748736 | bytes 20250624 | tf_op jit(solution)/shard_map/convert.6
  71.7 0.0 copy-done
  71.7 0.0 all-to-all-done.1
  71.8 0.2 copy.29
  71.9 0.2 dot_general.8
  72.1 8.2 %fusion.7 = bf16[2,24,3072]{2,1,0:T(8,128)(2,1)S(1)} fusion(bf16[2,24,3072]{2,1,0:T(8,128)(2,1)S(1)} %dot_general.8, bf16[3072,1536]{1,0:T(8,128)(2,1)} %bitcast.62, bf16[3072,1536]{1,0:T(8,128)(2,1)} %bitcast.60, f32[2,3072]{1,0:T(2,128)S(1)} %dynamic-slice_bitcast_fusion), kind=kOutput, calls=%fused_computation.10 | convolution fusion | flops 944013312 | bytes 19488768 | tf_op jit(solution)/shard_map/dot_general | solution.py:56
  80.3 9.6 %fusion.10 = bf16[48,3072]{1,0:T(8,128)(2,1)S(1)} fusion(bf16[48,3072]{1,0:T(8,128)(2,1)S(1)} %bitcast.73, bf16[3072,1536]{1,0:T(8,128)(2,1)} %bitcast.63, bf16[3072,1536]{1,0:T(8,128)(2,1)} %bitcast.61), kind=kOutput, calls=%fused_computation.11 | convolution fusion | flops 944013312 | bytes 19464192 | tf_op jit(solution)/shard_map/dot_general | solution.py:49
  90.0 1.9 %copy.26 = bf16[2,24,3072]{1,0,2:T(2,128)(2,1)S(1)} copy(bf16[2,24,3072]{2,1,0:T(8,128)(2,1)S(1)} %bitcast.69) | data formatting | bytes 589824 | tf_op jit(solution)/shard_map/reshape | solution.py:60
  91.9 2.6 %reshape.245 = bf16[4,2,18432]{2,1,0:T(2,128)(2,1)} reshape(bf16[3072,2,24]{2,1,0:T(2,128)(2,1)S(1)} %bitcast.64) | data formatting | bytes 589824
  94.5 4.8 %all-to-all-start.2 = ((bf16[4,2,18432]{2,1,0:T(2,128)(2,1)}), bf16[4,2,18432]{2,1,0:T(2,128)(2,1)S(1)}, u32[]{:S(2)}, u32[]{:S(2)}) async-start(bf16[4,2,18432]{2,1,0:T(2,128)(2,1)} %reshape.245), calls=%async_computation.2 | async-start | bytes 589824 | tf_op jit(solution)/shard_map/all_to_all | solution.py:102
  99.4 8.7 %all-to-all-done.2 = bf16[4,2,18432]{2,1,0:T(2,128)(2,1)S(1)} async-done(((bf16[4,2,18432]{2,1,0:T(2,128)(2,1)}), bf16[4,2,18432]{2,1,0:T(2,128)(2,1)S(1)}, u32[]{:S(2)}, u32[]{:S(2)}) %all-to-all-start.2) | async-done | bytes 294944 | tf_op jit(solution)/shard_map/all_to_all | solution.py:102
  108.1 3.1 %reshape.246 = bf16[3072,2,24]{2,1,0:T(2,128)(2,1)} reshape(bf16[4,2,18432]{2,1,0:T(2,128)(2,1)S(1)} %all-to-all-done.2) | data formatting | bytes 589824
  111.2 2.5 %convert_bitcast_fusion = f32[4,2,24,768]{2,1,3,0:T(2,128)S(1)} fusion(bf16[2,24,4,768]{1,0,3,2:T(2,128)(2,1)} %bitcast.65), kind=kLoop, calls=%fused_computation.12 | loop fusion | flops 147456 | bytes 884736 | tf_op jit(solution)/shard_map/convert_element_type | solution.py:103
  113.7 2.9 %copy.27 = f32[4,2,24,768]{3,2,1,0:T(8,128)} copy(f32[4,2,24,768]{2,1,3,0:T(2,128)S(1)} %convert_bitcast_fusion) | data formatting | bytes 1179648 | tf_op jit(solution)/shard_map/convert_element_type | solution.py:103
  116.5 1.2 fusion.31
  117.8 3.3 %collective-permute-start.2 = (bf16[8,1,768]{2,1,0:T(2,128)(2,1)S(1)}, bf16[8,1,768]{2,1,0:T(2,128)(2,1)S(1)}, u32[]{:S(2)}, u32[]{:S(2)}) collective-permute-start(bf16[8,1,768]{2,1,0:T(2,128)(2,1)S(1)} %get-tuple-element.10), channel_id=1, source_target_pairs={{4,0},{8,4},{12,8},{5,1},{9,5},{13,9},{6,2},{10,6},{14,10},{7,3},{... | collective-permute-start | bytes 36872 | tf_op jit(solution)/shard_map/ppermute | solution.py:18
  121.1 2.5 %collective-permute-start.1 = (bf16[8,1,768]{2,1,0:T(2,128)(2,1)S(1)}, bf16[8,1,768]{2,1,0:T(2,128)(2,1)S(1)}, u32[]{:S(2)}, u32[]{:S(2)}) collective-permute-start(bf16[8,1,768]{2,1,0:T(2,128)(2,1)S(1)} %get-tuple-element.9), channel_id=1, source_target_pairs={{0,4},{4,8},{8,12},{1,5},{5,9},{9,13},{2,6},{6,10},{10,14},{3,7},{... | collective-permute-start | bytes 36872 | tf_op jit(solution)/shard_map/ppermute | solution.py:15
  123.6 0.9 convert_select_fusion
  124.5 0.0 collective-permute-done.2
  124.5 3.2 %collective-permute-done.1 = bf16[8,1,768]{2,1,0:T(2,128)(2,1)S(1)} collective-permute-done((bf16[8,1,768]{2,1,0:T(2,128)(2,1)S(1)}, bf16[8,1,768]{2,1,0:T(2,128)(2,1)S(1)}, u32[]{:S(2)}, u32[]{:S(2)}) %collective-permute-start.1) | collective-permute-done | bytes 12320 | tf_op jit(solution)/shard_map/ppermute | solution.py:15
  127.7 0.1 maximum_convert_fusion
  127.9 2.2 %fusion.15 = f32[1,8,24,768]{3,2,1,0:T(8,128)} fusion(f32[8,26,768]{2,1,0:T(8,128)S(1)} %maximum_convert_fusion, f32[24,768]{1,0:T(8,128)S(1)} %convert_select_fusion, f32[24,768]{1,0:T(8,128)} %bitcast.71, f32[4,2,24,768]{3,2,1,0:T(8,128)} %copy.27, f32[4,24,768]{2,1,0:T(8,128)} %copy-done.1, f32[4,24,768]{2,1,0:T(8,128)S(1)} %copy.24), kind=kLoop, calls=%fused_computation.19 | loop fusion | flops 1179648 | bytes 3096576 | tf_op jit(solution)/shard_map/broadcast_in_dim | solution.py:105
  (8 shorter events, 0.1 us)
Async XLA Ops:
  0.0 71.7 %copy-start = (f32[1,8,3072]{2,1,0:T(8,128)S(1)}, f32[1,8,3072]{2,1,0:T(8,128)}, u32[]{:S(2)}) copy-start(f32[1,8,3072]{2,1,0:T(8,128)} %param.9) | copy-start | bytes 294916
  0.0 6.9 %copy-start.2 = (s32[1,1,1,16,128]{4,3,2,1,0:T(8,128)S(1)}, s32[1,1,1,16,128]{4,3,2,1,0:T(8,128)}, u32[]{:S(2)}) copy-start(s32[1,1,1,16,128]{4,3,2,1,0:T(8,128)} %param.12) | copy-start | bytes 24580
  0.0 16.3 %copy-start.3 = (f32[1,1,1,16,128]{4,3,2,1,0:T(8,128)S(1)}, f32[1,1,1,16,128]{4,3,2,1,0:T(8,128)}, u32[]{:S(2)}) copy-start(f32[1,1,1,16,128]{4,3,2,1,0:T(8,128)} %param.14) | copy-start | bytes 24580
  0.0 16.3 %copy-start.5 = (s32[1,1,1,16]{3,2,1,0:T(1,128)S(1)}, s32[1,1,1,16]{3,2,1,0:T(1,128)}, u32[]{:S(2)}) copy-start(s32[1,1,1,16]{3,2,1,0:T(1,128)} %param.15) | copy-start | bytes 196
  0.0 27.3 %copy-start.4 = (s32[1,1,1,16,128]{4,3,2,1,0:T(8,128)S(1)}, s32[1,1,1,16,128]{4,3,2,1,0:T(8,128)}, u32[]{:S(2)}) copy-start(s32[1,1,1,16,128]{4,3,2,1,0:T(8,128)} %param.13) | copy-start | bytes 24580
  1.2 56.6 %copy-start.1 = (f32[4,24,768]{2,1,0:T(8,128)}, f32[4,24,768]{2,1,0:T(8,128)S(1)}, u32[]{:S(2)}) copy-start(f32[4,24,768]{2,1,0:T(8,128)S(1)} %get-tuple-element.8) | copy-start | bytes 884740
  16.4 2.9 %collective-permute-start = (f32[16,4,128]{2,0,1:T(8,128)S(1)}, f32[16,4,128]{2,0,1:T(8,128)S(1)}, u32[]{:S(2)}, u32[]{:S(2)}) collective-permute-start(f32[16,4,128]{2,0,1:T(8,128)S(1)} %multiply_bitcast_fusion), channel_id=1, source_target_pairs={{0,16},{16,0},{1,17},{17,1},{2,18},{18,2},{3,19},{19,3},{4,20},{20... | collective-permute-start | bytes 98312 | tf_op jit(solution)/shard_map/ppermute | solution.py:26
  20.0 13.4 %all-to-all-start = ((f32[16,4,128]{2,1,0:T(4,128)}), f32[16,4,128]{2,1,0:T(4,128)S(1)}, u32[]{:S(2)}, u32[]{:S(2)}) async-start(f32[16,4,128]{2,1,0:T(4,128)} %copy.22), calls=%async_computation | async-start | bytes 65536 | tf_op jit(solution)/shard_map/all_to_all | solution.py:94
  58.5 13.2 %all-to-all-start.1 = ((bf16[8,24,768]{2,1,0:T(8,128)(2,1)}), bf16[8,24,768]{2,1,0:T(8,128)(2,1)S(1)}, u32[]{:S(2)}, u32[]{:S(2)}) async-start(bf16[8,24,768]{2,1,0:T(8,128)(2,1)} %fusion.16), calls=%async_computation.1 | async-start | bytes 589824 | tf_op jit(solution)/shard_map/all_to_all | solution.py:100
  94.5 13.5 %all-to-all-start.2 = ((bf16[4,2,18432]{2,1,0:T(2,128)(2,1)}), bf16[4,2,18432]{2,1,0:T(2,128)(2,1)S(1)}, u32[]{:S(2)}, u32[]{:S(2)}) async-start(bf16[4,2,18432]{2,1,0:T(2,128)(2,1)} %reshape.245), calls=%async_computation.2 | async-start | bytes 589824 | tf_op jit(solution)/shard_map/all_to_all | solution.py:102
  117.8 6.8 %collective-permute-start.2 = (bf16[8,1,768]{2,1,0:T(2,128)(2,1)S(1)}, bf16[8,1,768]{2,1,0:T(2,128)(2,1)S(1)}, u32[]{:S(2)}, u32[]{:S(2)}) collective-permute-start(bf16[8,1,768]{2,1,0:T(2,128)(2,1)S(1)} %get-tuple-element.10), channel_id=1, source_target_pairs={{4,0},{8,4},{12,8},{5,1},{9,5},{13,9},{6,2},{10,6},{14,10},{7,3},{... | collective-permute-start | bytes 36872 | tf_op jit(solution)/shard_map/ppermute | solution.py:18
  121.1 6.6 %collective-permute-start.1 = (bf16[8,1,768]{2,1,0:T(2,128)(2,1)S(1)}, bf16[8,1,768]{2,1,0:T(2,128)(2,1)S(1)}, u32[]{:S(2)}, u32[]{:S(2)}) collective-permute-start(bf16[8,1,768]{2,1,0:T(2,128)(2,1)S(1)} %get-tuple-element.9), channel_id=1, source_target_pairs={{0,4},{4,8},{8,12},{1,5},{5,9},{9,13},{2,6},{6,10},{10,14},{3,7},{... | collective-permute-start | bytes 36872 | tf_op jit(solution)/shard_map/ppermute | solution.py:15
where the time goes:
time: 131 us; the launch traced here: 130 us
  other arithmetic  37.8 us (29%)
  local copies, waits for them, and re-layouts  34.6 us (26%)
  starting transfers between devices  21.7 us (17%)
  waiting for transfers between devices  17.9 us (14%)
  matrix products  17.8 us (14%)
    scatter-add x1, other arithmetic, local(): surface = surface.at[:, dst_idx].add(incoming)  17.6 us
    dot_general x1, matrix products, back_transform(): lax.dot_general(filtered, table_part, (((1,), (1,)), ((), ())), preferred...  9.63 us
    another operation x1, other arithmetic  9.56 us
    gather x2, local copies, waits for them, and re-layouts, local(): outgoing = jnp.transpose(surface[:, src_idx] * weights[None], (1, 0, 2))  9.47 us
    all_to_all x1, waiting for transfers between devices, local(): incr = lax.all_to_all(incr, 'gy', split_axis=2, concat_axis=0, tiled=True)  8.68 us
    dot_general x1, matrix products, circle_increment(): jnp.dot(circles.reshape(-1, cols_all), table, preferred_element_type=jnp....  8.22 us
    all_to_all x1, starting transfers between devices, local(): lax.all_to_all(crossed, ('gx', 'gy'), split_axis=0, concat_axis=0, tiled=...  7.28 us
    slice x2, local copies, waits for them, and re-layouts, local(): surface = fields[:FC].reshape(FC, cells)  6.81 us
  transfers between devices with their start and end apart: 6, of which 3 were waited for; matrix products, arithmetic and copies ran while one was open for 10% of the time, Pallas kernels for 0%

commit v1 on v0

--- a/solution.py
+++ b/solution.py
@@ -1,10 +1,23 @@
+import functools
 import math
 import jax
 import jax.numpy as jnp
 from jax import lax
 from jax.sharding import PartitionSpec as P
+from jax.lax import all_to_all, axis_size
 
 FC = 4
+
+
+def track_axis_part(panel, along_dim, where_dim):
+    side_arr = jnp.concatenate(
+        all_to_all(jnp.stack(jnp.split(panel, axis_size("gy"), axis=along_dim)), "gy", 0, 0),
+        axis=where_dim,
+    )
+    return side_arr
+
+
+connect_streams = functools.partial(track_axis_part, along_dim=2, where_dim=0)
 
 
 def extended(block, sides, width):
@@ -99,7 +112,7 @@
     grid_bf = fields.astype(jnp.bfloat16)
     circles = lax.all_to_all(grid_bf, "gy", split_axis=0, concat_axis=2, tiled=True)
     incr = circle_increment(circles, resp_mine, table, scale)
-    incr = lax.all_to_all(incr, "gy", split_axis=2, concat_axis=0, tiled=True)
+    incr = connect_streams(incr)
     fields = fields + incr.astype(jnp.float32)
     fields = diffuse(fields, rate) * keep[None]
     return fields[None]

time: 131 us -> 116 us (0.89)
  local copies, waits for them, and re-layouts: 34.6 us -> 24.1 us
  other arithmetic: 37.8 us -> 32.6 us
    unnamed x14, local copies, waits for them, and re-layouts: 5.78 us -> 0.03 us
    convert_element_type x1 -> x0, local copies, waits for them, and re-layouts: 2.86 us -> none  [local(): fields = fields + incr.astype(jnp.float32)]
    convert_element_type x1 -> x0, other arithmetic: 2.49 us -> none  [local(): fields = fields + incr.astype(jnp.float32)]
    reshape x1 -> x0, local copies, waits for them, and re-layouts: 1.89 us -> none  [circle_increment(): return incr.reshape(count, rows_part, cols_all)]
    another operation x1 -> x2, other arithmetic: 9.56 us -> 9.99 us
  transfers between devices with their start and end apart: 6 -> 6, of which waited for: 3 -> 3; matrix products, arithmetic and copies ran while one was open for 10% -> 11% of each run, Pallas kernels for 0% -> 0%
where the time goes in v1:
time: 116 us; the launch traced here: 115 us
  other arithmetic  32.6 us (28%)
  local copies, waits for them, and re-layouts  24.1 us (21%)
  starting transfers between devices  21.7 us (19%)
  waiting for transfers between devices  18.8 us (16%)
  matrix products  17.9 us (15%)
    scatter-add x1, other arithmetic, local(): surface = surface.at[:, dst_idx].add(incoming)  17.6 us
    dot_general x1, matrix products, back_transform(): lax.dot_general(filtered, table_part, (((1,), (1,)), ((), ())), preferred...  9.66 us
    gather x2, local copies, waits for them, and re-layouts, local(): outgoing = jnp.transpose(surface[:, src_idx] * weights[None], (1, 0, 2))  9.47 us
    another operation x1, other arithmetic  9.23 us
    all_to_all x1, waiting for transfers between devices, track_axis_part(): all_to_all(jnp.stack(jnp.split(panel, axis_size('gy'), axis=along_dim)),...  8.68 us
    dot_general x1, matrix products, circle_increment(): jnp.dot(circles.reshape(-1, cols_all), table, preferred_element_type=jnp....  8.21 us
    all_to_all x1, starting transfers between devices, local(): lax.all_to_all(crossed, ('gx', 'gy'), split_axis=0, concat_axis=0, tiled=...  7.28 us
    slice x2, local copies, waits for them, and re-layouts, local(): surface = fields[:FC].reshape(FC, cells)  6.8 us
  transfers between devices with their start and end apart: 6, of which 3 were waited for; matrix products, arithmetic and copies ran while one was open for 11% of the time, Pallas kernels for 0%

profile of v1, /device:TPU:4, one launch (start us, length us, event | category | flops | bytes accessed | tf_op | source)
XLA Modules:
  0.0 115.3 jit_solution(15895539600735677836)
XLA Ops:
  0.0 0.0 copy-start
  0.0 0.0 copy-start.3
  0.0 0.0 copy-start.4
  0.0 0.0 copy-start.6
  0.0 0.0 copy-start.5
  0.0 1.1 fusion.37
  1.2 5.7 %copy.17 = f32[1,4,24,768]{1,3,2,0:T(8,128)} copy(f32[1,4,24,768]{3,2,1,0:T(8,128)S(1)} %get-tuple-element.7) | data formatting | bytes 589824 | tf_op jit(solution)/shard_map/slice | solution.py:104
  6.8 0.0 copy-done.3
  6.8 9.1 %gather_fusion = f32[2048,4]{1,0:T(8,128)S(1)} fusion(f32[4,18432]{0,1:T(8,128)} %bitcast.57, s32[2048]{0:T(1024)S(1)} %fusion.34), kind=kCustom, calls=%fused_computation | custom fusion | bytes 73728 | tf_op jit(solution)/shard_map/gather | solution.py:105
  16.0 0.3 copy.18
  16.3 0.0 copy-done.4
  16.3 0.0 copy-done.6
  16.3 0.1 bitcast_select_fusion
  16.4 0.1 collective-permute-start
  16.5 1.3 %fusion.30 = (f32[48,1536]{1,0:T(8,128)S(1)}, f32[48,1536]{1,0:T(8,128)S(1)}) fusion(s32[48]{0:T(128)S(1)} %iota_multiply_fusion), kind=kLoop, calls=%fused_computation.41 | loop fusion | flops 663552 | bytes 590016 | tf_op jit(solution)/shard_map/cos | solution.py:49
  17.8 1.6 %fusion.21 = (f32[64,1536]{1,0:T(8,128)S(1)}, f32[64,1536]{1,0:T(8,128)S(1)}) fusion(), kind=kLoop, calls=%fused_computation.29 | loop fusion | flops 884736 | bytes 786432 | tf_op jit(solution)/shard_map/sin | solution.py:49
  19.4 0.0 collective-permute-done
  19.4 0.6 copy.19
  20.0 7.3 %all-to-all-start = ((f32[16,4,128]{2,1,0:T(4,128)}), f32[16,4,128]{2,1,0:T(4,128)S(1)}, u32[]{:S(2)}, u32[]{:S(2)}) async-start(f32[16,4,128]{2,1,0:T(4,128)} %copy.19), calls=%async_computation | async-start | bytes 65536 | tf_op jit(solution)/shard_map/all_to_all | solution.py:107
  27.3 0.0 copy-done.5
  27.3 6.1 %all-to-all-done = f32[16,4,128]{2,1,0:T(4,128)S(1)} async-done(((f32[16,4,128]{2,1,0:T(4,128)}), f32[16,4,128]{2,1,0:T(4,128)S(1)}, u32[]{:S(2)}, u32[]{:S(2)}) %all-to-all-start) | async-done | bytes 32800 | tf_op jit(solution)/shard_map/all_to_all | solution.py:107
  33.4 0.4 copy.20
  33.7 17.6 %scatter_fusion = f32[4,18432]{0,1:T(8,128)} fusion(f32[4,18432]{0,1:T(8,128)} %bitcast.58, s32[2048]{0:T(1024)S(1)} %fusion.32, f32[2048,4]{1,0:T(8,128)S(1)} %copy.20), kind=kCustom, calls=%fused_computation.1 | custom fusion | flops 8192 | bytes 106496 | tf_op jit(solution)/shard_map/scatter-add | solution.py:109
  51.4 6.4 %copy.21 = f32[4,24,768]{2,1,0:T(8,128)S(1)} copy(f32[4,24,768]{0,2,1:T(8,128)} %bitcast.59) | data formatting | bytes 589824 | tf_op jit(solution)/shard_map/reshape | solution.py:110
  57.8 0.8 fusion.16
  58.5 3.5 %all-to-all-start.1 = ((bf16[8,24,768]{2,1,0:T(8,128)(2,1)}), bf16[8,24,768]{2,1,0:T(8,128)(2,1)S(1)}, u32[]{:S(2)}, u32[]{:S(2)}) async-start(bf16[8,24,768]{2,1,0:T(8,128)(2,1)} %fusion.16), calls=%async_computation.1 | async-start | bytes 589824 | tf_op jit(solution)/shard_map/all_to_all | solution.py:113
  62.0 9.2 %subtract_convert_fusion = (bf16[48,64,1536]{2,1,0:T(8,128)(2,1)}, bf16[48,64,1536]{2,1,0:T(8,128)(2,1)}) fusion(f32[64,1536]{1,0:T(8,128)S(1)} %get-tuple-element.17, f32[48,1536]{1,0:T(8,128)S(1)} %get-tuple-element.16, f32[64,1536]{1,0:T(8,128)S(1)} %get-tuple-element.18, f32[48,1536]{1,0:T(8,128)S(1)} %get-tuple-element.15), kind=kLoop, calls=%fused_computation.6 | loop fusion | flops 37748736 | bytes 20250624 | tf_op jit(solution)/shard_map/convert.4
  71.2 0.0 copy-done
  71.2 0.0 all-to-all-done.1
  71.2 0.2 copy.24
  71.4 0.2 dot_general.8
  71.6 8.2 %fusion.7 = bf16[2,24,3072]{2,1,0:T(8,128)(2,1)S(1)} fusion(bf16[2,24,3072]{2,1,0:T(8,128)(2,1)S(1)} %dot_general.8, bf16[3072,1536]{1,0:T(8,128)(2,1)} %bitcast.62, bf16[3072,1536]{1,0:T(8,128)(2,1)} %bitcast.60, f32[2,3072]{1,0:T(2,128)S(1)} %dynamic-slice_bitcast_fusion), kind=kOutput, calls=%fused_computation.10 | convolution fusion | flops 944013312 | bytes 19488768 | tf_op jit(solution)/shard_map/dot_general | solution.py:69
  79.8 0.0 copy-start.2
  79.8 0.0 copy-start.1
  79.8 9.7 %fusion.10 = bf16[48,3072]{1,0:T(8,128)(2,1)S(1)} fusion(bf16[48,3072]{1,0:T(8,128)(2,1)S(1)} %bitcast.71, bf16[3072,1536]{1,0:T(8,128)(2,1)} %bitcast.63, bf16[3072,1536]{1,0:T(8,128)(2,1)} %bitcast.61), kind=kOutput, calls=%fused_computation.11 | convolution fusion | flops 944013312 | bytes 19464192 | tf_op jit(solution)/shard_map/dot_general | solution.py:62
  89.5 0.8 pad_maximum_fusion.8
  90.3 5.0 %all-to-all-start.2 = ((bf16[4,2,24,768]{3,2,1,0:T(8,128)(2,1)}), bf16[4,2,24,768]{3,2,1,0:T(8,128)(2,1)S(1)}, u32[]{:S(2)}, u32[]{:S(2)}) async-start(bf16[4,2,24,768]{3,2,1,0:T(8,128)(2,1)} %pad_maximum_fusion.8), calls=%async_computation.2 | async-start | bytes 589824 | tf_op jit(solution)/shard_map/all_to_all | solution.py:14
  95.3 8.7 %all-to-all-done.2 = bf16[4,2,24,768]{3,2,1,0:T(8,128)(2,1)S(1)} async-done(((bf16[4,2,24,768]{3,2,1,0:T(8,128)(2,1)}), bf16[4,2,24,768]{3,2,1,0:T(8,128)(2,1)S(1)}, u32[]{:S(2)}, u32[]{:S(2)}) %all-to-all-start.2) | async-done | bytes 294944 | tf_op jit(solution)/shard_map/all_to_all | solution.py:14
  104.0 0.1 fusion.24
  104.1 3.3 %collective-permute-start.2 = (bf16[8,1,768]{2,1,0:T(2,128)(2,1)S(1)}, bf16[8,1,768]{2,1,0:T(2,128)(2,1)S(1)}, u32[]{:S(2)}, u32[]{:S(2)}) collective-permute-start(bf16[8,1,768]{2,1,0:T(2,128)(2,1)S(1)} %get-tuple-element.10), channel_id=1, source_target_pairs={{4,0},{8,4},{12,8},{5,1},{9,5},{13,9},{6,2},{10,6},{14,10},{7,3},{... | collective-permute-start | bytes 36872 | tf_op jit(solution)/shard_map/ppermute | solution.py:31
  107.5 2.5 %collective-permute-start.1 = (bf16[8,1,768]{2,1,0:T(2,128)(2,1)S(1)}, bf16[8,1,768]{2,1,0:T(2,128)(2,1)S(1)}, u32[]{:S(2)}, u32[]{:S(2)}) collective-permute-start(bf16[8,1,768]{2,1,0:T(2,128)(2,1)S(1)} %get-tuple-element.9), channel_id=1, source_target_pairs={{0,4},{4,8},{8,12},{1,5},{5,9},{9,13},{2,6},{6,10},{10,14},{3,7},{... | collective-permute-start | bytes 36872 | tf_op jit(solution)/shard_map/ppermute | solution.py:28
  110.0 0.0 copy-done.2
  110.0 0.0 collective-permute-done.2
  110.0 4.0 %collective-permute-done.1 = bf16[8,1,768]{2,1,0:T(2,128)(2,1)S(1)} collective-permute-done((bf16[8,1,768]{2,1,0:T(2,128)(2,1)S(1)}, bf16[8,1,768]{2,1,0:T(2,128)(2,1)S(1)}, u32[]{:S(2)}, u32[]{:S(2)}) %collective-permute-start.1) | collective-permute-done | bytes 12320 | tf_op jit(solution)/shard_map/ppermute | solution.py:28
  114.1 0.1 maximum_convert_fusion
  114.2 0.0 copy-done.1
  114.2 1.0 fusion.15
  (8 shorter events, 0.1 us)
Async XLA Ops:
  0.0 71.2 %copy-start = (f32[1,8,3072]{2,1,0:T(8,128)S(1)}, f32[1,8,3072]{2,1,0:T(8,128)}, u32[]{:S(2)}) copy-start(f32[1,8,3072]{2,1,0:T(8,128)} %param.9) | copy-start | bytes 294916
  0.0 6.8 %copy-start.3 = (s32[1,1,1,16,128]{4,3,2,1,0:T(8,128)S(1)}, s32[1,1,1,16,128]{4,3,2,1,0:T(8,128)}, u32[]{:S(2)}) copy-start(s32[1,1,1,16,128]{4,3,2,1,0:T(8,128)} %param.12) | copy-start | bytes 24580
  0.0 16.3 %copy-start.4 = (f32[1,1,1,16,128]{4,3,2,1,0:T(8,128)S(1)}, f32[1,1,1,16,128]{4,3,2,1,0:T(8,128)}, u32[]{:S(2)}) copy-start(f32[1,1,1,16,128]{4,3,2,1,0:T(8,128)} %param.14) | copy-start | bytes 24580
  0.0 16.3 %copy-start.6 = (s32[1,1,1,16]{3,2,1,0:T(1,128)S(1)}, s32[1,1,1,16]{3,2,1,0:T(1,128)}, u32[]{:S(2)}) copy-start(s32[1,1,1,16]{3,2,1,0:T(1,128)} %param.15) | copy-start | bytes 196
  0.0 27.3 %copy-start.5 = (s32[1,1,1,16,128]{4,3,2,1,0:T(8,128)S(1)}, s32[1,1,1,16,128]{4,3,2,1,0:T(8,128)}, u32[]{:S(2)}) copy-start(s32[1,1,1,16,128]{4,3,2,1,0:T(8,128)} %param.13) | copy-start | bytes 24580
  16.4 2.9 %collective-permute-start = (f32[16,4,128]{2,0,1:T(8,128)S(1)}, f32[16,4,128]{2,0,1:T(8,128)S(1)}, u32[]{:S(2)}, u32[]{:S(2)}) collective-permute-start(f32[16,4,128]{2,0,1:T(8,128)S(1)} %multiply_bitcast_fusion), channel_id=1, source_target_pairs={{0,16},{16,0},{1,17},{17,1},{2,18},{18,2},{3,19},{19,3},{4,20},{20... | collective-permute-start | bytes 98312 | tf_op jit(solution)/shard_map/ppermute | solution.py:39
  20.0 13.4 %all-to-all-start = ((f32[16,4,128]{2,1,0:T(4,128)}), f32[16,4,128]{2,1,0:T(4,128)S(1)}, u32[]{:S(2)}, u32[]{:S(2)}) async-start(f32[16,4,128]{2,1,0:T(4,128)} %copy.19), calls=%async_computation | async-start | bytes 65536 | tf_op jit(solution)/shard_map/all_to_all | solution.py:107
  58.5 12.7 %all-to-all-start.1 = ((bf16[8,24,768]{2,1,0:T(8,128)(2,1)}), bf16[8,24,768]{2,1,0:T(8,128)(2,1)S(1)}, u32[]{:S(2)}, u32[]{:S(2)}) async-start(bf16[8,24,768]{2,1,0:T(8,128)(2,1)} %fusion.16), calls=%async_computation.1 | async-start | bytes 589824 | tf_op jit(solution)/shard_map/all_to_all | solution.py:113
  79.8 30.2 %copy-start.2 = (s32[24,768]{1,0:T(8,128)S(1)}, s32[24,768]{1,0:T(8,128)}, u32[]{:S(2)}) copy-start(s32[24,768]{1,0:T(8,128)} %param.11) | copy-start | bytes 221188
  79.8 34.4 %copy-start.1 = (f32[1,24,768]{2,1,0:T(8,128)S(1)}, f32[1,24,768]{2,1,0:T(8,128)}, u32[]{:S(2)}) copy-start(f32[1,24,768]{2,1,0:T(8,128)} %param.10) | copy-start | bytes 221188
  90.3 13.7 %all-to-all-start.2 = ((bf16[4,2,24,768]{3,2,1,0:T(8,128)(2,1)}), bf16[4,2,24,768]{3,2,1,0:T(8,128)(2,1)S(1)}, u32[]{:S(2)}, u32[]{:S(2)}) async-start(bf16[4,2,24,768]{3,2,1,0:T(8,128)(2,1)} %pad_maximum_fusion.8), calls=%async_computation.2 | async-start | bytes 589824 | tf_op jit(solution)/shard_map/all_to_all | solution.py:14
  104.1 5.9 %collective-permute-start.2 = (bf16[8,1,768]{2,1,0:T(2,128)(2,1)S(1)}, bf16[8,1,768]{2,1,0:T(2,128)(2,1)S(1)}, u32[]{:S(2)}, u32[]{:S(2)}) collective-permute-start(bf16[8,1,768]{2,1,0:T(2,128)(2,1)S(1)} %get-tuple-element.10), channel_id=1, source_target_pairs={{4,0},{8,4},{12,8},{5,1},{9,5},{13,9},{6,2},{10,6},{14,10},{7,3},{... | collective-permute-start | bytes 36872 | tf_op jit(solution)/shard_map/ppermute | solution.py:31
  107.5 6.6 %collective-permute-start.1 = (bf16[8,1,768]{2,1,0:T(2,128)(2,1)S(1)}, bf16[8,1,768]{2,1,0:T(2,128)(2,1)S(1)}, u32[]{:S(2)}, u32[]{:S(2)}) collective-permute-start(bf16[8,1,768]{2,1,0:T(2,128)(2,1)S(1)} %get-tuple-element.9), channel_id=1, source_target_pairs={{0,4},{4,8},{8,12},{1,5},{5,9},{9,13},{2,6},{6,10},{10,14},{3,7},{... | collective-permute-start | bytes 36872 | tf_op jit(solution)/shard_map/ppermute | solution.py:28
